TPU v7x, 128 devices: a whole 4x4x4 slice. The times are simulated.
128 devices in a mesh: dp: 8 (over z_lo, y), sp: 16 (over x, z_hi, core).
Axes of the slice: x: 4, y: 4, z: 4 (z_hi: 2, z_lo: 2; z = z_hi * 2 + z_lo), core: 2. Of those that a mesh axis runs over, the one named last changes fastest.
Arguments:
- feats: bfloat16 [8, 32, 256, 128], P('dp', None, 'sp'), may hold values from -62 to 62
- conv_w: bfloat16 [1152, 256], replicated, may hold values from -0.1875 to 0.1875
- group_norm_gain: float32 [256], replicated, may hold values from 0.5 to 1.5
- group_norm_bias: float32 [256], replicated, may hold values from -3 to 3
- emb_w: bfloat16 [256, 3072], replicated, may hold values from -0.375 to 0.375
- time_w: bfloat16 [256, 9216], replicated, may hold values from -0.375 to 0.375
- up_w: bfloat16 [3072, 6144], P(None, 'sp'), may hold values from -0.109375 to 0.109375
- down_w: bfloat16 [6144, 3072], P('sp'), may hold values from -0.078125 to 0.078125
- steps: int32 [8], P('dp'), may hold values from 0 to 999
- cotangent: bfloat16 [8, 2048, 3072], P('dp', 'sp'), may hold values from -28 to 28
Outputs:
- grad_conv: float32 [1152, 256], replicated
- grad_up: float32 [3072, 6144], P('dp', 'sp')
- grad_down: float32 [6144, 3072], P('sp', 'dp')
All inputs are finite; a program needn't handle non-finite values.
Results may differ from a plain program's by a relative error of at most 0.012.
Values may be sent and summed in bfloat16 or wider, within the bound.
A program may use at most 192 MiB of HBM per device.

v0:
```python
import math
import jax
import jax.numpy as jnp
from jax import lax
from jax.sharding import Mesh
from jax.sharding import PartitionSpec as P

NORM_GROUPS = 32
SP = ("sp_0", "sp_1", "sp_2")
DP_SP = ("dp", "sp_0", "sp_1", "sp_2")


def from_behind(array, axis, by):
    length = lax.axis_size(axis)
    pairs = [(i, i + by) for i in range(length) if 0 <= i + by < length]
    return lax.ppermute(array, axis, pairs)


def copy_for_each(array, axis):
    length = lax.axis_size(axis)
    return lax.all_to_all(
        jnp.broadcast_to(array[None], (length, *array.shape)), axis, 0, 0, tiled=True
    )


def over_copies(array, axis):
    return copy_for_each(array, axis).sum(axis=0)


def in_one(arrays, axis):
    ends = [0]
    for a in arrays:
        ends.append(ends[-1] + a.size)
    subtotal = over_copies(jnp.concatenate([a.ravel() for a in arrays]), axis)
    return tuple((subtotal[b:e].reshape(a.shape) for a, b, e in zip(arrays, ends, ends[1:])))


def side_by_side(arrays, axis, dim, along):
    both = jnp.concatenate(arrays, axis=along)
    filled, at, finished = (lax.all_gather(both, axis, axis=dim, tiled=True), 0, [])
    for a in arrays:
        finished.append(lax.slice_in_dim(filled, at, at + a.shape[along], axis=along))
        at += a.shape[along]
    return tuple(finished)


def in_blocks(array, dim, length):
    before, after = (array.shape[:dim], array.shape[dim + 1 :])
    return jnp.moveaxis(array.reshape(*before, length, -1, *after), dim, 0)


def sum_by_chip(array, chips, core, dim):
    sizes = (lax.axis_size(chips), lax.axis_size(core))
    parts = in_blocks(array, dim, sizes[0] * sizes[1])
    inside = parts.shape[1:]
    parts = parts.reshape(*sizes, *inside).swapaxes(0, 1).reshape(-1, *inside)
    parts = lax.psum_scatter(parts, core, scatter_dimension=0, tiled=True)
    return lax.psum_scatter(parts, chips, scatter_dimension=0, tiled=True)[0]


def sum_packed(arrays, axis, dims):
    length = lax.axis_size(axis)
    parts = [in_blocks(a, dim, length) for a, dim in zip(arrays, dims)]
    lines = jnp.concatenate([b.reshape(length, -1) for b in parts], axis=1)
    rows = max(16, -(-lines.shape[1] // 1024) * 8)
    lines = jnp.pad(lines, ((0, 0), (0, rows * 128 - lines.shape[1]))).reshape(-1, 128)
    ravelled, at, finished = (lax.psum_scatter(lines, axis, tiled=True).reshape(-1), 0, [])
    for b in parts:
        part = b[0]
        finished.append(ravelled[at : at + part.size].reshape(part.shape))
        at += part.size
    return tuple(finished)


def gelu_pair(u):
    coef = math.sqrt(2.0 / math.pi)
    inner = coef * (u + 0.044715 * u * u * u)
    tangent = jnp.tanh(inner)
    value = 0.5 * u * (1.0 + tangent)
    slope = 0.5 * (1.0 + tangent) + 0.5 * u * (1.0 - tangent * tangent) * coef * (
        1.0 + 3.0 * 0.044715 * u * u
    )
    return (value, slope)


def silu_pair(value):
    sigma = jax.nn.sigmoid(value)
    return (value * sigma, sigma * (1.0 + value * (1.0 - sigma)))


def modulation(step_value, time_w):
    half = time_w.shape[0] // 2
    freqs = jnp.exp(-math.log(10000.0) * jnp.arange(half, dtype=jnp.float32) / half)
    angle = step_value.astype(jnp.float32) * freqs
    embed = jnp.concatenate([jnp.cos(angle), jnp.sin(angle)])
    mixed = jnp.dot(
        jax.nn.silu(embed).astype(jnp.bfloat16)[None, :], time_w, preferred_element_type=jnp.float32
    )[0]
    width = time_w.shape[1] // 3
    return (mixed[:width], mixed[width : 2 * width], mixed[2 * width :])


def make_patches(padded, rows, cols):
    pieces = []
    for row_tap in range(3):
        for col_tap in range(3):
            pieces.append(
                padded[row_tap : row_tap + 2 * rows : 2, col_tap : col_tap + 2 * cols : 2, :]
            )
    stacked = jnp.concatenate(pieces, axis=-1)
    return stacked.reshape(rows * cols, stacked.shape[-1])


def group_totals(first, second, groups):
    tokens, width = first.shape
    first_g = first.reshape(tokens, groups, width // groups)
    second_g = second.reshape(tokens, groups, width // groups)
    return (jnp.sum(first_g, axis=(0, 2)), jnp.sum(second_g, axis=(0, 2)))


def broadcast_groups(values, width):
    return jnp.repeat(values, width // values.shape[0])


def contract(left, right, left_dim, right_dim):
    return lax.dot_general(
        left, right, (((left_dim,), (right_dim,)), ((), ())), preferred_element_type=jnp.float32
    )


def on_device(
    feats, conv_w, group_norm_gain, group_norm_bias, emb_w, time_w, up_w, down_w, steps, cotangent
):
    devices_sp = lax.axis_size(SP)
    image = feats[0]
    rows_in, cols_in, _ = image.shape
    rows = rows_in // 2
    cols = cols_in // 2
    seq_rows = rows // devices_sp
    channel_count = conv_w.shape[1]
    rim = from_behind(image[:, cols_in - 1, :], SP, 1)
    widened = jnp.concatenate([rim[:, None, :], image], axis=1)
    padded = jnp.pad(widened, ((1, 0), (0, 0), (0, 0)))
    patches = make_patches(padded, rows, cols)
    normed_value = jnp.dot(patches, conv_w, preferred_element_type=jnp.float32)
    first, second = group_totals(normed_value, normed_value * normed_value, NORM_GROUPS)
    first, second = in_one((first, second), SP)
    group_count = normed_value.shape[0] * devices_sp * (channel_count // NORM_GROUPS)
    group_mean = first / group_count
    rstd = lax.rsqrt(second / group_count - group_mean * group_mean + 1e-05)
    channel_rstd = broadcast_groups(rstd, channel_count)
    centered_input = (normed_value - broadcast_groups(group_mean, channel_count)) * channel_rstd
    preactivation = centered_input * group_norm_gain + group_norm_bias
    act_val, silu_slope = silu_pair(preactivation)
    act_b = act_val.astype(jnp.bfloat16)
    shift, scale, gate = modulation(steps[0], time_w)
    cot_seq = cotangent[0]
    moved = lax.all_to_all(
        act_b.reshape(rows, cols, channel_count), SP, split_axis=0, concat_axis=1, tiled=True
    )
    local_act = moved.reshape(seq_rows * cols * devices_sp, channel_count)
    hidden_in = jnp.dot(local_act, emb_w, preferred_element_type=jnp.float32)
    centered = hidden_in - jnp.mean(hidden_in, axis=-1, keepdims=True)
    token_rstd = lax.rsqrt(jnp.mean(centered * centered, axis=-1, keepdims=True) + 1e-06)
    hhat = centered * token_rstd
    normed = (hhat * (1.0 + scale) + shift).astype(jnp.bfloat16)
    all_normed, all_cot = side_by_side((normed, cot_seq), SP, 0, 1)
    upper = jnp.dot(all_normed, up_w, preferred_element_type=jnp.float32)
    gelu_val, gelu_slope = gelu_pair(upper)
    hid = gelu_val.astype(jnp.bfloat16)
    scaled_cot = (all_cot.astype(jnp.float32) * gate).astype(jnp.bfloat16)
    dhid = contract(scaled_cot, down_w, 1, 1)
    dupper = (dhid * gelu_slope).astype(jnp.bfloat16)
    dnormed = sum_by_chip(
        contract(dupper, up_w, 1, 1).astype(jnp.bfloat16), ("sp_0", "sp_1"), "sp_2", 0
    ).astype(jnp.float32)
    grad_up_local = contract(all_normed, dupper, 0, 0)
    grad_down_local = contract(hid, scaled_cot, 0, 0)
    grad_up, grad_down = tuple(
        (
            part.astype(jnp.float32)
            for part in sum_packed(
                (grad_up_local.astype(jnp.bfloat16), grad_down_local.astype(jnp.bfloat16)),
                "dp",
                (0, 1),
            )
        )
    )
    dhh = dnormed * (1.0 + scale)
    dhh_mean = jnp.mean(dhh, axis=-1, keepdims=True)
    dhh_cross = jnp.mean(dhh * hhat, axis=-1, keepdims=True)
    dh_val = (
        cot_seq.astype(jnp.float32) + token_rstd * (dhh - dhh_mean - hhat * dhh_cross)
    ).astype(jnp.bfloat16)
    dact = contract(dh_val, emb_w, 1, 1)
    back_tiles = lax.all_to_all(
        dact.reshape(seq_rows, cols * devices_sp, channel_count).astype(jnp.bfloat16),
        SP,
        split_axis=1,
        concat_axis=0,
        tiled=True,
    ).astype(jnp.float32)
    dact_tile = back_tiles.reshape(rows * cols, channel_count)
    input_gradient = dact_tile * silu_slope * group_norm_gain
    backward_first, backward_second = group_totals(
        input_gradient, input_gradient * centered_input, NORM_GROUPS
    )
    backward_first, backward_second = in_one((backward_first, backward_second), SP)
    normed_gradient = (
        channel_rstd
        * (
            input_gradient
            - broadcast_groups(backward_first / group_count, channel_count)
            - centered_input * broadcast_groups(backward_second / group_count, channel_count)
        )
    ).astype(jnp.bfloat16)
    conv_local = contract(patches, normed_gradient, 0, 0)
    grad_conv = lax.psum(conv_local, DP_SP)
    return (grad_conv, grad_up, grad_down)


def solution(mesh):
    finer = Mesh(mesh.devices.reshape(mesh.shape["dp"], 4, 2, 2), ("dp", "sp_0", "sp_1", "sp_2"))
    in_specs = (
        P("dp", None, SP, None),
        P(),
        P(),
        P(),
        P(),
        P(),
        P(None, SP),
        P(SP, None),
        P("dp"),
        P("dp", SP, None),
    )
    out_specs = (P(), P("dp", SP), P(SP, "dp"))
    return jax.shard_map(
        on_device, mesh=finer, in_specs=in_specs, out_specs=out_specs, check_vma=False
    )
```

profile of v0, /device:TPU:1, one launch (start us, length us, event | category | flops | bytes accessed | tf_op | source)
XLA Modules:
  0.0 589.0 jit_solution(9743201290991420241)
XLA Ops:
  8.3 6.9 %collective-permute-start = (bf16[32,128]{1,0:T(8,128)(2,1)S(1)}, bf16[32,128]{1,0:T(8,128)(2,1)S(1)}, u32[]{:S(2)}, u32[]{:S(2)}) collective-permute-start(bf16[32,128]{1,0:T(8,128)(2,1)S(1)} %slice_bitcast_fusion), channel_id=1, source_target_pairs={{0,1},{1,2},{2,3},{3,4},{4,5},{5,6},{6,7},{7,8},{8,9},{9,10},{10,1... | collective-permute-start | bytes 24584 | tf_op jit(solution)/shard_map/ppermute | solution.py:16
  21.0 7.9 %all-to-all-start = ((f32[16,1,64]{2,1,0:T(1,128)}), f32[16,1,64]{2,1,0:T(1,128)S(1)}, u32[]{:S(2)}, u32[]{:S(2)}) async-start(f32[16,1,64]{2,1,0:T(1,128)} %broadcast_in_dim.15), calls=%async_computation | async-start | bytes 16384 | tf_op jit(solution)/shard_map/all_to_all | solution.py:21
  29.0 3.1 fusion.66
  32.0 3.9 all-to-all-done
  37.0 4.0 all-to-all-start.1
  41.0 7.4 %all-to-all-done.1 = bf16[16,8,256]{2,1,0:T(8,128)(2,1)S(1)} async-done(((bf16[16,8,256]{2,1,0:T(8,128)(2,1)}), bf16[16,8,256]{2,1,0:T(8,128)(2,1)S(1)}, u32[]{:S(2)}, u32[]{:S(2)}) %all-to-all-start.1) | async-done | bytes 65568 | tf_op jit(solution)/shard_map/all_to_all | solution.py:158
  48.4 1.9 fusion.65
  53.5 146.6 %all-gather.2.cloned.1.call-done = bf16[2048,6144]{1,0:T(8,128)(2,1)} async-done(((bf16[128,6144]{1,0:T(8,128)(2,1)}), bf16[2048,6144]{1,0:T(8,128)(2,1)}) %all-gather.2.cloned.1.call-update) | async-done | bytes 25165840 | tf_op jit(solution)/shard_map/all_gather | solution.py:40
  200.1 9.7 %fusion.2 = f32[2048,384]{1,0:T(8,128)S(1)} fusion(bf16[3072,384]{1,0:T(8,128)(2,1)S(1)} %copy-done, bf16[2048,6144]{1,0:T(8,128)(2,1)} %all-gather.2.cloned.1.call-done), kind=kOutput, calls=%fused_computation.4 | convolution fusion | flops 4831838208 | bytes 18087936 | tf_op jit(solution)/shard_map/dot_general | solution.py:168
  209.9 12.3 %fusion.16 = bf16[2048,384]{1,0:T(8,128)(2,1)S(1)} fusion(f32[2048,384]{1,0:T(8,128)S(1)} %fusion.2, bf16[384,3072]{1,0:T(8,128)(2,1)S(1)} %copy-done.8, bf16[2048,6144]{1,0:T(8,128)(2,1)} %all-gather.2.cloned.1.call-done, f32[3072]{0:T(1024)S(1)} %get-tuple-element.12), kind=kOutput, calls=%fused_computation.19 | convolution fusion | flops 4865654784 | bytes 19673088 | tf_op jit(solution)/shard_map/dot_general | solution.py:126
  222.2 7.0 %convolution_convert_fusion = bf16[2048,3072]{1,0:T(8,128)(2,1)S(1)} fusion(bf16[2048,384]{1,0:T(8,128)(2,1)S(1)} %fusion.16, bf16[3072,384]{1,0:T(8,128)(2,1)S(1)} %copy-done), kind=kOutput, calls=%fused_computation.1 | convolution fusion | flops 4838129664 | bytes 16515072 | tf_op jit(solution)/shard_map/dot_general | solution.py:126
  229.3 5.4 copy.33
  236.0 10.8 %fusion.7 = bf16[3072,384]{1,0:T(8,128)(2,1)} fusion(bf16[2048,384]{1,0:T(8,128)(2,1)S(1)} %copy-done.10, bf16[2048,6144]{1,0:T(8,128)(2,1)} %all-gather.2.cloned.1.call-done), kind=kOutput, calls=%fused_computation.12 | convolution fusion | flops 4833017856 | bytes 16515072 | tf_op jit(solution)/shard_map/dot_general | solution.py:126
  246.8 3.2 reshape_reshape.7
  250.0 13.4 %fusion.6 = bf16[384,3072]{1,0:T(8,128)(2,1)S(1)} fusion(bf16[2048,6144]{1,0:T(8,128)(2,1)} %all-gather.2.cloned.1.call-done, f32[3072]{0:T(1024)S(1)} %get-tuple-element.12, f32[2048,384]{1,0:T(8,128)} %copy-done.11), kind=kOutput, calls=%fused_computation.11 | convolution fusion | flops 4858970112 | bytes 18100224 | tf_op jit(solution)/shard_map/dot_general | solution.py:126
  265.7 10.4 %pad_maximum_fusion = bf16[8,294912]{1,0:T(8,128)(2,1)} fusion(bf16[8,147456]{1,0:T(8,128)(2,1)} %bitcast.67, bf16[8,147456]{1,0:T(8,128)(2,1)S(1)} %reshape_reshape.7), kind=kLoop, calls=%fused_computation.10 | loop fusion | flops 9437184 | bytes 9437184 | tf_op jit(solution)/shard_map/concatenate | solution.py:64
  276.1 6.6 %reshape.118 = bf16[18432,128]{1,0:T(8,128)(2,1)} reshape(bf16[8,294912]{1,0:T(8,128)(2,1)} %pad_maximum_fusion) | data formatting | bytes 9437184 | tf_op jit(solution)/shard_map/reshape | solution.py:66
  282.8 79.5 %reduce-scatter.6.cloned.1.call-done = bf16[1,128,3072]{2,1,0:T(8,128)(2,1)} async-done(((bf16[8,128,3072]{2,1,0:T(8,128)(2,1)}), bf16[1,128,3072]{2,1,0:T(8,128)(2,1)}) %reduce-scatter.6.cloned.1.call-update) | async-done | bytes 786448 | tf_op jit(solution)/shard_map/reduce_scatter | solution.py:58
  364.0 2.5 fusion.29
  368.1 12.2 %all_to_all.30 = bf16[16,2,1024]{2,1,0:T(2,128)(2,1)S(1)} all-to-all(bf16[16,2,1024]{2,1,0:T(2,128)(2,1)S(1)} %reshape.125), channel_id=1, replica_groups=mesh['dp'=8,'sp_0'=4,'sp_1'=2,'sp_2'=2] {'sp_0','sp_1','sp_2'}, dimensions={0} | all-to-all | bytes 131072 | tf_op jit(solution)/shard_map/all_to_all | solution.py:196
  381.0 10.0 %all_to_all.31 = f32[16,1,64]{2,1,0:T(1,128)S(1)} all-to-all(f32[16,1,64]{2,1,0:T(1,128)S(1)} %broadcast_in_dim.18), channel_id=1, replica_groups=mesh['dp'=8,'sp_0'=4,'sp_1'=2,'sp_2'=2] {'sp_0','sp_1','sp_2'}, dimensions={0} | all-to-all | bytes 8192 | tf_op jit(solution)/shard_map/all_to_all | solution.py:21
  392.9 29.4 %reduce-scatter.8.cloned.1.call-done = bf16[2304,128]{1,0:T(8,128)(2,1)} async-done(((bf16[18432,128]{1,0:T(8,128)(2,1)}), bf16[2304,128]{1,0:T(8,128)(2,1)}) %reduce-scatter.8.cloned.1.call-update) | async-done | bytes 589840 | tf_op jit(solution)/shard_map/reduce_scatter | solution.py:67
  425.3 154.8 %all-reduce.3.cloned.1.call-done = f32[1152,256]{1,0:T(8,128)} async-done(((f32[1152,256]{1,0:T(8,128)}), f32[1152,256]{1,0:T(8,128)}) %all-reduce.3.cloned.1.call-update) | async-done | bytes 1179664 | tf_op jit(solution)/shard_map/psum | solution.py:218
  580.2 2.4 copy.64
  (106 shorter events, 22.9 us)
Async XLA Ops:
  7.2 193.0 %copy-start = (bf16[3072,384]{1,0:T(8,128)(2,1)S(1)}, bf16[3072,384]{1,0:T(8,128)(2,1)}, u32[]{:S(2)}) copy-start(bf16[3072,384]{1,0:T(8,128)(2,1)} %param.16) | copy-start | bytes 7077892
  8.3 7.7 %collective-permute-start = (bf16[32,128]{1,0:T(8,128)(2,1)S(1)}, bf16[32,128]{1,0:T(8,128)(2,1)S(1)}, u32[]{:S(2)}, u32[]{:S(2)}) collective-permute-start(bf16[32,128]{1,0:T(8,128)(2,1)S(1)} %slice_bitcast_fusion), channel_id=1, source_target_pairs={{0,1},{1,2},{2,3},{3,4},{4,5},{5,6},{6,7},{7,8},{8,9},{9,10},{10,1... | collective-permute-start | bytes 24584 | tf_op jit(solution)/shard_map/ppermute | solution.py:16
  18.5 17.8 %copy-start.6 = (f32[256]{0:T(256)S(1)}, f32[256]{0:T(256)}, u32[]{:S(2)}) copy-start(f32[256]{0:T(256)} %param.13) | copy-start | bytes 3076
  18.5 17.8 %copy-start.7 = (f32[256]{0:T(256)S(1)}, f32[256]{0:T(256)}, u32[]{:S(2)}) copy-start(f32[256]{0:T(256)} %param.12) | copy-start | bytes 3076
  21.0 14.8 %all-to-all-start = ((f32[16,1,64]{2,1,0:T(1,128)}), f32[16,1,64]{2,1,0:T(1,128)S(1)}, u32[]{:S(2)}, u32[]{:S(2)}) async-start(f32[16,1,64]{2,1,0:T(1,128)} %broadcast_in_dim.15), calls=%async_computation | async-start | bytes 16384 | tf_op jit(solution)/shard_map/all_to_all | solution.py:21
  37.0 11.4 %all-to-all-start.1 = ((bf16[16,8,256]{2,1,0:T(8,128)(2,1)}), bf16[16,8,256]{2,1,0:T(8,128)(2,1)S(1)}, u32[]{:S(2)}, u32[]{:S(2)}) async-start(bf16[16,8,256]{2,1,0:T(8,128)(2,1)} %fusion.52), calls=%async_computation.1 | async-start | bytes 131072 | tf_op jit(solution)/shard_map/all_to_all | solution.py:158
  41.0 159.2 %all-gather.2.cloned.1.call-start = ((), (), s32[]{:S(2)}) async-start(), calls=%async_computation.7 | async-start | bytes 26738688 | tf_op jit(solution)/shard_map/all_gather | solution.py:40
  48.4 3.5 copy-start.4
  50.4 1.2 copy-start.2
  53.3 212.1 %reduce-scatter.4.cloned.1.call-start = ((), (), s32[]{:S(2)}) async-start(), calls=%async_computation.8 | async-start | bytes 18874368 | tf_op jit(solution)/shard_map/reduce_scatter | solution.py:57
  200.1 9.8 %copy-start.8 = (bf16[384,3072]{1,0:T(8,128)(2,1)S(1)}, bf16[384,3072]{1,0:T(8,128)(2,1)}, u32[]{:S(2)}) copy-start(bf16[384,3072]{1,0:T(8,128)(2,1)} %param.17) | copy-start | bytes 7077892
  209.9 12.3 %copy-start.11 = (f32[2048,384]{1,0:T(8,128)}, f32[2048,384]{1,0:T(8,128)S(1)}, u32[]{:S(2)}) copy-start(f32[2048,384]{1,0:T(8,128)S(1)} %fusion.2) | copy-start | bytes 9437188
  222.2 7.0 %copy-start.9 = (bf16[2048,384]{1,0:T(8,128)(2,1)}, bf16[2048,384]{1,0:T(8,128)(2,1)S(1)}, u32[]{:S(2)}) copy-start(bf16[2048,384]{1,0:T(8,128)(2,1)S(1)} %fusion.16) | copy-start | bytes 4718596
  234.6 1.4 copy-start.10
  234.6 127.7 %reduce-scatter.6.cloned.1.call-start = ((), (), s32[]{:S(2)}) async-start(), calls=%async_computation.9 | async-start | bytes 7077888 | tf_op jit(solution)/shard_map/reduce_scatter | solution.py:58
  265.4 156.9 %reduce-scatter.8.cloned.1.call-start = ((), (), s32[]{:S(2)}) async-start(), calls=%async_computation.11 | async-start | bytes 5308416 | tf_op jit(solution)/shard_map/reduce_scatter | solution.py:67
  282.7 79.6 %copy-start.3 = (f32[128,3072]{1,0:T(8,128)S(1)}, f32[128,3072]{1,0:T(8,128)}, u32[]{:S(2)}) copy-start(f32[128,3072]{1,0:T(8,128)} %copy-done.2) | copy-start | bytes 4718596
  282.7 81.2 %copy-start.5 = (bf16[1,128,3072]{2,1,0:T(8,128)(2,1)S(1)}, bf16[1,128,3072]{2,1,0:T(8,128)(2,1)}, u32[]{:S(2)}) copy-start(bf16[1,128,3072]{2,1,0:T(8,128)(2,1)} %param.19) | copy-start | bytes 2359300
  282.7 297.4 %all-reduce.3.cloned.1.call-start = ((), (), s32[]{:S(2)}) async-start(), calls=%async_computation.10 | async-start | bytes 2359296 | tf_op jit(solution)/shard_map/psum | solution.py:218
  392.8 189.7 %copy-start.1 = (bf16[3072,384]{1,0:T(8,128)(2,1)S(1)}, bf16[3072,384]{1,0:T(8,128)(2,1)}, u32[]{:S(2)}) copy-start(bf16[3072,384]{1,0:T(8,128)(2,1)} %param.16) | copy-start | bytes 7077892
Sparse Core Ops, SparseCore 0:
  53.4 146.6 all-gather.1
  234.8 21.5 reduce-scatter.3
  265.5 96.7 reduce-scatter.5
  364.7 57.5 reduce-scatter.7
  428.2 151.9 all-reduce.2
where the time goes:
time: 590 us; the launch traced here: 589 us
  waiting for transfers between devices  422 us (72%)
  matrix products  63.3 us (11%)
  local copies, waits for them, and re-layouts  29.3 us (5%)
  blocking collectives  22.2 us (4%)
  starting transfers between devices  19.6 us (3%)
  other arithmetic  17.9 us (3%)
  between operations  14.8 us (3%)
    psum x1, waiting for transfers between devices, on_device(): grad_conv = lax.psum(conv_local, DP_SP)  155 us
    all_gather x1, waiting for transfers between devices, side_by_side(): lax.all_gather(both, axis, axis=dim, tiled=True)  147 us
    reduce_scatter x1, waiting for transfers between devices, sum_by_chip(): return lax.psum_scatter(parts, chips, scatter_dimension=0, tiled=True)[0]  79.5 us
    dot_general x6, matrix products, contract(): lax.dot_general(left, right, (((left_dim,), (right_dim,)), ((), ())), pre...  47.3 us
    reduce_scatter x1, waiting for transfers between devices, sum_packed(): lax.psum_scatter(lines, axis, tiled=True).reshape(-1)  29.4 us
    all_to_all x1, blocking collectives, on_device(): lax.all_to_all(dact.reshape(seq_rows, cols * devices_sp, channel_count).a...  12.2 us
  transfers between devices with their start and end apart: 8, of which 6 were waited for; matrix products, arithmetic and copies ran while one was open for 10% of the time, Pallas kernels for 0%

commit v1 on v0

--- a/solution.py
+++ b/solution.py
@@ -4,10 +4,15 @@
 from jax import lax
 from jax.sharding import Mesh
 from jax.sharding import PartitionSpec as P
+from jax.lax import all_to_all, axis_size
 
 NORM_GROUPS = 32
 SP = ("sp_0", "sp_1", "sp_2")
 DP_SP = ("dp", "sp_0", "sp_1", "sp_2")
+patch_put = lambda inp, lane_axis, d0, dimension_no: jnp.concatenate(
+    all_to_all(jnp.stack(jnp.split(inp, axis_size(lane_axis), d0), axis=0), lane_axis, 0, 0),
+    dimension_no,
+)
 
 
 def from_behind(array, axis, by):
@@ -193,12 +198,11 @@
         cot_seq.astype(jnp.float32) + token_rstd * (dhh - dhh_mean - hhat * dhh_cross)
     ).astype(jnp.bfloat16)
     dact = contract(dh_val, emb_w, 1, 1)
-    back_tiles = lax.all_to_all(
+    back_tiles = patch_put(
         dact.reshape(seq_rows, cols * devices_sp, channel_count).astype(jnp.bfloat16),
-        SP,
-        split_axis=1,
-        concat_axis=0,
-        tiled=True,
+        lane_axis=SP,
+        d0=1,
+        dimension_no=0,
     ).astype(jnp.float32)
     dact_tile = back_tiles.reshape(rows * cols, channel_count)
     input_gradient = dact_tile * silu_slope * group_norm_gain

time: 590 us -> 589 us (level)
  no operation moved by 1% of the time
where the time goes in v1:
time: 589 us
  waiting for transfers between devices  423 us (72%)
  matrix products  63.4 us (11%)
  local copies, waits for them, and re-layouts  28.6 us (5%)
  blocking collectives  21.9 us (4%)
  starting transfers between devices  19.6 us (3%)
  other arithmetic  16.9 us (3%)
  between operations  14.9 us (3%)
    psum x1, waiting for transfers between devices, on_device(): grad_conv = lax.psum(conv_local, DP_SP)  155 us
    all_gather x1, waiting for transfers between devices, side_by_side(): lax.all_gather(both, axis, axis=dim, tiled=True)  147 us
    reduce_scatter x1, waiting for transfers between devices, sum_by_chip(): return lax.psum_scatter(parts, chips, scatter_dimension=0, tiled=True)[0]  79.7 us
    dot_general x6, matrix products, contract(): lax.dot_general(left, right, (((left_dim,), (right_dim,)), ((), ())), pre...  47.3 us
    reduce_scatter x1, waiting for transfers between devices, sum_packed(): lax.psum_scatter(lines, axis, tiled=True).reshape(-1)  31.1 us
    all_to_all x1, blocking collectives, all_to_all(jnp.stack(jnp.split(inp, axis_size(lane_axis), d0), axis=0), l...  11.9 us
  transfers between devices with their start and end apart: 8, of which 6 were waited for; matrix products, arithmetic and copies ran while one was open for 10% of the time, Pallas kernels for 0%

profile of v1, /device:TPU:1, one launch (start us, length us, event | category | flops | bytes accessed | tf_op | source)
XLA Modules:
  0.0 588.8 jit_solution(800800306029763828)
XLA Ops:
  8.3 6.9 %collective-permute-start = (bf16[32,128]{1,0:T(8,128)(2,1)S(1)}, bf16[32,128]{1,0:T(8,128)(2,1)S(1)}, u32[]{:S(2)}, u32[]{:S(2)}) collective-permute-start(bf16[32,128]{1,0:T(8,128)(2,1)S(1)} %slice_bitcast_fusion), channel_id=1, source_target_pairs={{0,1},{1,2},{2,3},{3,4},{4,5},{5,6},{6,7},{7,8},{8,9},{9,10},{10,1... | collective-permute-start | bytes 24584 | tf_op jit(solution)/shard_map/ppermute | solution.py:21
  21.0 7.9 %all-to-all-start = ((f32[16,1,64]{2,1,0:T(1,128)}), f32[16,1,64]{2,1,0:T(1,128)S(1)}, u32[]{:S(2)}, u32[]{:S(2)}) async-start(f32[16,1,64]{2,1,0:T(1,128)} %broadcast_in_dim.15), calls=%async_computation | async-start | bytes 16384 | tf_op jit(solution)/shard_map/all_to_all | solution.py:26
  29.0 3.1 fusion.66
  32.0 3.9 all-to-all-done
  37.0 4.0 all-to-all-start.1
  41.0 7.4 %all-to-all-done.1 = bf16[16,8,256]{2,1,0:T(8,128)(2,1)S(1)} async-done(((bf16[16,8,256]{2,1,0:T(8,128)(2,1)}), bf16[16,8,256]{2,1,0:T(8,128)(2,1)S(1)}, u32[]{:S(2)}, u32[]{:S(2)}) %all-to-all-start.1) | async-done | bytes 65568 | tf_op jit(solution)/shard_map/all_to_all | solution.py:163
  48.4 1.9 fusion.65
  53.5 146.6 %all-gather.2.cloned.1.call-done = bf16[2048,6144]{1,0:T(8,128)(2,1)} async-done(((bf16[128,6144]{1,0:T(8,128)(2,1)}), bf16[2048,6144]{1,0:T(8,128)(2,1)}) %all-gather.2.cloned.1.call-update) | async-done | bytes 25165840 | tf_op jit(solution)/shard_map/all_gather | solution.py:45
  200.1 9.8 %fusion.2 = f32[2048,384]{1,0:T(8,128)S(1)} fusion(bf16[3072,384]{1,0:T(8,128)(2,1)S(1)} %copy-done, bf16[2048,6144]{1,0:T(8,128)(2,1)} %all-gather.2.cloned.1.call-done), kind=kOutput, calls=%fused_computation.4 | convolution fusion | flops 4831838208 | bytes 18087936 | tf_op jit(solution)/shard_map/dot_general | solution.py:173
  209.9 12.3 %fusion.16 = bf16[2048,384]{1,0:T(8,128)(2,1)S(1)} fusion(f32[2048,384]{1,0:T(8,128)S(1)} %fusion.2, bf16[384,3072]{1,0:T(8,128)(2,1)S(1)} %copy-done.8, bf16[2048,6144]{1,0:T(8,128)(2,1)} %all-gather.2.cloned.1.call-done, f32[3072]{0:T(1024)S(1)} %get-tuple-element.11), kind=kOutput, calls=%fused_computation.19 | convolution fusion | flops 4865654784 | bytes 19673088 | tf_op jit(solution)/shard_map/dot_general | solution.py:131
  222.2 7.0 %convolution_convert_fusion = bf16[2048,3072]{1,0:T(8,128)(2,1)S(1)} fusion(bf16[2048,384]{1,0:T(8,128)(2,1)S(1)} %fusion.16, bf16[3072,384]{1,0:T(8,128)(2,1)S(1)} %copy-done), kind=kOutput, calls=%fused_computation.1 | convolution fusion | flops 4838129664 | bytes 16515072 | tf_op jit(solution)/shard_map/dot_general | solution.py:131
  229.3 5.4 copy.26
  236.0 10.8 %fusion.7 = bf16[3072,384]{1,0:T(8,128)(2,1)} fusion(bf16[2048,384]{1,0:T(8,128)(2,1)S(1)} %copy-done.10, bf16[2048,6144]{1,0:T(8,128)(2,1)} %all-gather.2.cloned.1.call-done), kind=kOutput, calls=%fused_computation.12 | convolution fusion | flops 4833017856 | bytes 16515072 | tf_op jit(solution)/shard_map/dot_general | solution.py:131
  246.8 3.2 reshape_reshape.7
  250.1 13.4 %fusion.6 = bf16[384,3072]{1,0:T(8,128)(2,1)S(1)} fusion(bf16[2048,6144]{1,0:T(8,128)(2,1)} %all-gather.2.cloned.1.call-done, f32[3072]{0:T(1024)S(1)} %get-tuple-element.11, f32[2048,384]{1,0:T(8,128)} %copy-done.11), kind=kOutput, calls=%fused_computation.11 | convolution fusion | flops 4858970112 | bytes 18100224 | tf_op jit(solution)/shard_map/dot_general | solution.py:131
  265.7 10.4 %pad_maximum_fusion = bf16[8,294912]{1,0:T(8,128)(2,1)} fusion(bf16[8,147456]{1,0:T(8,128)(2,1)} %bitcast.133, bf16[8,147456]{1,0:T(8,128)(2,1)S(1)} %reshape_reshape.7), kind=kLoop, calls=%fused_computation.10 | loop fusion | flops 9437184 | bytes 9437184 | tf_op jit(solution)/shard_map/concatenate | solution.py:69
  276.1 6.6 %reshape.116 = bf16[18432,128]{1,0:T(8,128)(2,1)} reshape(bf16[8,294912]{1,0:T(8,128)(2,1)} %pad_maximum_fusion) | data formatting | bytes 9437184 | tf_op jit(solution)/shard_map/reshape | solution.py:71
  282.8 79.7 %reduce-scatter.6.cloned.1.call-done = bf16[1,128,3072]{2,1,0:T(8,128)(2,1)} async-done(((bf16[8,128,3072]{2,1,0:T(8,128)(2,1)}), bf16[1,128,3072]{2,1,0:T(8,128)(2,1)}) %reduce-scatter.6.cloned.1.call-update) | async-done | bytes 786448 | tf_op jit(solution)/shard_map/reduce_scatter | solution.py:63
  364.1 2.5 fusion.29
  366.8 11.9 %all_to_all.26 = bf16[16,1,8,256]{3,2,1,0:T(8,128)(2,1)S(1)} all-to-all(bf16[16,1,8,256]{3,2,1,0:T(8,128)(2,1)S(1)} %constant_dynamic-update-slice_fusion.9), channel_id=1, replica_groups=mesh['dp'=8,'sp_0'=4,'sp_1'=2,'sp_2'=2] {'sp_0','sp_1','sp_2'}, dimensions={0} | all-to-all | bytes 131072 | tf_op jit(solution)/shard_map/all_to_all | solution.py:13
  379.3 10.0 %all_to_all.27 = f32[16,1,64]{2,1,0:T(1,128)S(1)} all-to-all(f32[16,1,64]{2,1,0:T(1,128)S(1)} %broadcast_in_dim.18), channel_id=1, replica_groups=mesh['dp'=8,'sp_0'=4,'sp_1'=2,'sp_2'=2] {'sp_0','sp_1','sp_2'}, dimensions={0} | all-to-all | bytes 8192 | tf_op jit(solution)/shard_map/all_to_all | solution.py:26
  391.1 31.1 %reduce-scatter.8.cloned.1.call-done = bf16[2304,128]{1,0:T(8,128)(2,1)} async-done(((bf16[18432,128]{1,0:T(8,128)(2,1)}), bf16[2304,128]{1,0:T(8,128)(2,1)}) %reduce-scatter.8.cloned.1.call-update) | async-done | bytes 589840 | tf_op jit(solution)/shard_map/reduce_scatter | solution.py:72
  425.3 154.6 %all-reduce.3.cloned.1.call-done = f32[1152,256]{1,0:T(8,128)} async-done(((f32[1152,256]{1,0:T(8,128)}), f32[1152,256]{1,0:T(8,128)}) %all-reduce.3.cloned.1.call-update) | async-done | bytes 1179664 | tf_op jit(solution)/shard_map/psum | solution.py:222
  579.9 2.4 copy.66
  (117 shorter events, 21.3 us)
Async XLA Ops:
  7.2 193.0 %copy-start = (bf16[3072,384]{1,0:T(8,128)(2,1)S(1)}, bf16[3072,384]{1,0:T(8,128)(2,1)}, u32[]{:S(2)}) copy-start(bf16[3072,384]{1,0:T(8,128)(2,1)} %param.16) | copy-start | bytes 7077892
  8.3 7.7 %collective-permute-start = (bf16[32,128]{1,0:T(8,128)(2,1)S(1)}, bf16[32,128]{1,0:T(8,128)(2,1)S(1)}, u32[]{:S(2)}, u32[]{:S(2)}) collective-permute-start(bf16[32,128]{1,0:T(8,128)(2,1)S(1)} %slice_bitcast_fusion), channel_id=1, source_target_pairs={{0,1},{1,2},{2,3},{3,4},{4,5},{5,6},{6,7},{7,8},{8,9},{9,10},{10,1... | collective-permute-start | bytes 24584 | tf_op jit(solution)/shard_map/ppermute | solution.py:21
  18.5 17.8 %copy-start.6 = (f32[256]{0:T(256)S(1)}, f32[256]{0:T(256)}, u32[]{:S(2)}) copy-start(f32[256]{0:T(256)} %param.13) | copy-start | bytes 3076
  18.5 17.8 %copy-start.7 = (f32[256]{0:T(256)S(1)}, f32[256]{0:T(256)}, u32[]{:S(2)}) copy-start(f32[256]{0:T(256)} %param.12) | copy-start | bytes 3076
  21.0 14.8 %all-to-all-start = ((f32[16,1,64]{2,1,0:T(1,128)}), f32[16,1,64]{2,1,0:T(1,128)S(1)}, u32[]{:S(2)}, u32[]{:S(2)}) async-start(f32[16,1,64]{2,1,0:T(1,128)} %broadcast_in_dim.15), calls=%async_computation | async-start | bytes 16384 | tf_op jit(solution)/shard_map/all_to_all | solution.py:26
  37.0 11.4 %all-to-all-start.1 = ((bf16[16,8,256]{2,1,0:T(8,128)(2,1)}), bf16[16,8,256]{2,1,0:T(8,128)(2,1)S(1)}, u32[]{:S(2)}, u32[]{:S(2)}) async-start(bf16[16,8,256]{2,1,0:T(8,128)(2,1)} %fusion.52), calls=%async_computation.1 | async-start | bytes 131072 | tf_op jit(solution)/shard_map/all_to_all | solution.py:163
  41.0 159.2 %all-gather.2.cloned.1.call-start = ((), (), s32[]{:S(2)}) async-start(), calls=%async_computation.7 | async-start | bytes 26738688 | tf_op jit(solution)/shard_map/all_gather | solution.py:45
  48.4 3.5 copy-start.4
  50.4 1.2 copy-start.2
  53.3 212.1 %reduce-scatter.4.cloned.1.call-start = ((), (), s32[]{:S(2)}) async-start(), calls=%async_computation.8 | async-start | bytes 18874368 | tf_op jit(solution)/shard_map/reduce_scatter | solution.py:62
  200.1 9.8 %copy-start.8 = (bf16[384,3072]{1,0:T(8,128)(2,1)S(1)}, bf16[384,3072]{1,0:T(8,128)(2,1)}, u32[]{:S(2)}) copy-start(bf16[384,3072]{1,0:T(8,128)(2,1)} %param.17) | copy-start | bytes 7077892
  209.9 12.3 %copy-start.11 = (f32[2048,384]{1,0:T(8,128)}, f32[2048,384]{1,0:T(8,128)S(1)}, u32[]{:S(2)}) copy-start(f32[2048,384]{1,0:T(8,128)S(1)} %fusion.2) | copy-start | bytes 9437188
  222.2 7.0 %copy-start.9 = (bf16[2048,384]{1,0:T(8,128)(2,1)}, bf16[2048,384]{1,0:T(8,128)(2,1)S(1)}, u32[]{:S(2)}) copy-start(bf16[2048,384]{1,0:T(8,128)(2,1)S(1)} %fusion.16) | copy-start | bytes 4718596
  234.6 1.4 copy-start.10
  234.7 127.8 %reduce-scatter.6.cloned.1.call-start = ((), (), s32[]{:S(2)}) async-start(), calls=%async_computation.9 | async-start | bytes 7077888 | tf_op jit(solution)/shard_map/reduce_scatter | solution.py:63
  265.4 156.8 %reduce-scatter.8.cloned.1.call-start = ((), (), s32[]{:S(2)}) async-start(), calls=%async_computation.11 | async-start | bytes 5308416 | tf_op jit(solution)/shard_map/reduce_scatter | solution.py:72
  282.7 79.8 %copy-start.3 = (f32[128,3072]{1,0:T(8,128)S(1)}, f32[128,3072]{1,0:T(8,128)}, u32[]{:S(2)}) copy-start(f32[128,3072]{1,0:T(8,128)} %copy-done.2) | copy-start | bytes 4718596
  282.7 81.4 %copy-start.5 = (bf16[1,128,3072]{2,1,0:T(8,128)(2,1)S(1)}, bf16[1,128,3072]{2,1,0:T(8,128)(2,1)}, u32[]{:S(2)}) copy-start(bf16[1,128,3072]{2,1,0:T(8,128)(2,1)} %param.19) | copy-start | bytes 2359300
  282.7 297.1 %all-reduce.3.cloned.1.call-start = ((), (), s32[]{:S(2)}) async-start(), calls=%async_computation.10 | async-start | bytes 2359296 | tf_op jit(solution)/shard_map/psum | solution.py:222
  391.1 191.1 %copy-start.1 = (bf16[3072,384]{1,0:T(8,128)(2,1)S(1)}, bf16[3072,384]{1,0:T(8,128)(2,1)}, u32[]{:S(2)}) copy-start(bf16[3072,384]{1,0:T(8,128)(2,1)} %param.16) | copy-start | bytes 7077892
Sparse Core Ops, SparseCore 0:
  53.4 146.6 all-gather.1
  234.8 21.5 reduce-scatter.3
  265.5 96.9 reduce-scatter.5
  364.9 57.2 reduce-scatter.7
  428.1 151.7 all-reduce.2
